TPU v7x, 32 devices: a whole 2x2x4 slice. The times are simulated.
32 devices in a mesh: row: 8 (over z, y), col: 4 (over x, core).
Axes of the slice: x: 2, y: 2, z: 4, core: 2. Of those that a mesh axis runs over, the one named last changes fastest.
Arguments:
- orbitals: bfloat16 [20480, 384], P(('row', 'col')), may hold values from -6 to 6
- coulomb: float32 [20480, 20480], P('row', 'col'), may hold values from -0.001953125 to 0.001953125
- interp: bfloat16 [4096, 20480], P('row', 'col'), may hold values from -0.0390625 to 0.0390625
Outputs:
- exchanged: bfloat16 [4096, 384], P(('row', 'col'))
All inputs are finite; a program needn't handle non-finite values.
Results may differ from a plain program's by a relative error of at most 0.018.
Values may be sent and summed in bfloat16 or wider, within the bound.
No kernel may reach another device: no remote copies, remote signals or barrier semaphores. Data moves between devices by JAX's collectives and lax.ppermute only.
A program may use at most 128 MiB of HBM per device.

v0:
```python
import jax
import jax.numpy as jnp
from jax import lax
from jax.sharding import PartitionSpec as P


def broadcast(value, axis, source):
    kept = jnp.where(lax.axis_index(axis) == source, value, 0).astype(value.dtype)
    return lax.psum(kept, axis)


def local(orbitals, coulomb, interp):
    near = lax.all_gather(orbitals, "col", axis=0, tiled=True)
    factor = lax.axis_size("row") // lax.axis_size("col")
    column = lax.axis_index("col")
    pieces = []
    for offset in range(factor):
        pieces.append(broadcast(near, "row", column * factor + offset))
    far = jnp.concatenate(pieces, 0)
    density = lax.dot_general(
        near, far, (((1,), (1,)), ((), ())), preferred_element_type=jnp.float32
    )
    weighted = (coulomb * density).astype(jnp.bfloat16)
    partial_sum = lax.dot_general(
        weighted, near, (((0,), (0,)), ((), ())), preferred_element_type=jnp.float32
    )
    share = lax.psum_scatter(partial_sum, "row", scatter_dimension=0, tiled=True).astype(
        jnp.bfloat16
    )
    contracted = lax.all_gather(share, "row", axis=0, tiled=True)
    terms = jnp.dot(interp, contracted, preferred_element_type=jnp.float32)
    return lax.psum_scatter(terms.astype(jnp.bfloat16), "col", scatter_dimension=0, tiled=True)


def solution(mesh):
    in_specs = (P(("row", "col"), None), P("row", "col"), P("row", "col"))
    out_specs = P(("row", "col"), None)
    return jax.shard_map(local, mesh=mesh, in_specs=in_specs, out_specs=out_specs, check_vma=False)
```

profile of v0, /device:TPU:0, one launch (start us, length us, event | category | flops | bytes accessed | tf_op | source)
XLA Modules:
  0.0 489.1 jit_solution(2194609867817106554)
XLA Ops:
  6.5 0.0 all-gather.3.cloned.1.call-start
  6.5 0.7 all-gather.3.cloned.1.call-update
  7.3 0.0 all-reduce.3.cloned.1.call-start
  7.3 26.2 %all-gather.3.cloned.1.call-done = bf16[2560,384]{1,0:T(8,128)(2,1)} async-done(((bf16[640,384]{1,0:T(8,128)(2,1)}), bf16[2560,384]{1,0:T(8,128)(2,1)}) %all-gather.3.cloned.1.call-update) | async-done | bytes 1966096 | tf_op jit(solution)/shard_map/all_gather | solution.py:13
  33.5 0.0 copy-start
  33.5 4.0 broadcast_select_fusion.1
  37.5 0.0 all-reduce.3.cloned.1.call-update
  37.5 0.0 reduce-scatter.5.cloned.1.call-start
  37.5 149.6 %all-reduce.3.cloned.1.call-done = (bf16[2560,384]{1,0:T(8,128)(2,1)}, bf16[2560,384]{1,0:T(8,128)(2,1)}) async-done(((bf16[2560,384]{1,0:T(8,128)(2,1)}, bf16[2560,384]{1,0:T(8,128)(2,1)}), (bf16[2560,384]{1,0:T(8,128)(2,1)}, bf16[2560,384]{1,0:T(8,128)(2,1)})) %all-reduce.3.cloned.1.call-update) | async-done | bytes 3932176 | tf_op jit(solution)/shard_map/psum | solution.py:9
  187.1 0.0 copy-done
  187.1 58.8 %fusion.1 = f32[5120,384]{1,0:T(8,128)} fusion(bf16[2560,384]{1,0:T(8,128)(2,1)S(1)} %copy-done, f32[2560,5120]{1,0:T(8,128)} %param.4, bf16[2560,384]{1,0:T(8,128)(2,1)} %get-tuple-element.5, bf16[2560,384]{1,0:T(8,128)(2,1)} %get-tuple-element.6), kind=kOutput, calls=%fused_computation.2 | convolution fusion | flops 20166737920 | bytes 66191360 | tf_op jit(solution)/shard_map/dot_general | solution.py:24
  245.9 0.0 reduce-scatter.5.cloned.1.call-update
  246.0 0.0 all-gather.5.cloned.1.call-start
  246.0 139.4 %reduce-scatter.5.cloned.1.call-done = f32[640,384]{1,0:T(8,128)} async-done(((f32[5120,384]{1,0:T(8,128)}), f32[640,384]{1,0:T(8,128)}) %reduce-scatter.5.cloned.1.call-update) | async-done | bytes 983056 | tf_op jit(solution)/shard_map/reduce_scatter | solution.py:27
  385.4 2.0 convert_element_type.16
  387.4 0.0 all-gather.5.cloned.1.call-update
  387.4 0.2 reduce-scatter.7.cloned.1.call-start
  387.7 68.5 %all-gather.5.cloned.1.call-done = bf16[5120,384]{1,0:T(8,128)(2,1)} async-done(((bf16[640,384]{1,0:T(8,128)(2,1)}), bf16[5120,384]{1,0:T(8,128)(2,1)}) %all-gather.5.cloned.1.call-update) | async-done | bytes 3932176 | tf_op jit(solution)/shard_map/all_gather | solution.py:30
  456.2 5.9 %fusion.8 = bf16[512,384]{0,1:T(8,128)(2,1)S(1)} fusion(bf16[5120,384]{1,0:T(8,128)(2,1)} %all-gather.5.cloned.1.call-done, bf16[512,5120]{1,0:T(8,128)(2,1)} %param.5), kind=kOutput, calls=%fused_computation.9 | convolution fusion | flops 2013462528 | bytes 9568256 | tf_op jit(solution)/shard_map/dot_general | solution.py:31
  462.1 0.9 copy.6
  463.0 0.0 reduce-scatter.7.cloned.1.call-update
  463.0 19.6 %reduce-scatter.7.cloned.1.call-done = bf16[128,384]{1,0:T(8,128)(2,1)} async-done(((bf16[512,384]{1,0:T(8,128)(2,1)}), bf16[128,384]{1,0:T(8,128)(2,1)}) %reduce-scatter.7.cloned.1.call-update) | async-done | bytes 98320 | tf_op jit(solution)/shard_map/reduce_scatter | solution.py:32
Async XLA Ops:
  6.5 26.9 %all-gather.3.cloned.1.call-start = ((), (), s32[]{:S(2)}) async-start(), calls=%async_computation.2 | async-start | bytes 2457600 | tf_op jit(solution)/shard_map/all_gather | solution.py:13
  7.3 179.8 %all-reduce.3.cloned.1.call-start = ((), (), s32[]{:S(2)}) async-start(), calls=%async_computation.6 | async-start | bytes 7864320 | tf_op jit(solution)/shard_map/psum | solution.py:9
  33.5 153.6 %copy-start = (bf16[2560,384]{1,0:T(8,128)(2,1)S(1)}, bf16[2560,384]{1,0:T(8,128)(2,1)}, u32[]{:S(2)}) copy-start(bf16[2560,384]{1,0:T(8,128)(2,1)} %all-gather.3.cloned.1.call-done) | copy-start | bytes 5898244
  37.5 347.9 %reduce-scatter.5.cloned.1.call-start = ((), (), s32[]{:S(2)}) async-start(), calls=%async_computation.3 | async-start | bytes 8847360 | tf_op jit(solution)/shard_map/reduce_scatter | solution.py:27
  246.0 210.2 %all-gather.5.cloned.1.call-start = ((), (), s32[]{:S(2)}) async-start(), calls=%async_computation.4 | async-start | bytes 4423680 | tf_op jit(solution)/shard_map/all_gather | solution.py:30
  387.4 95.2 %reduce-scatter.7.cloned.1.call-start = ((), (), s32[]{:S(2)}) async-start(), calls=%async_computation.5 | async-start | bytes 491520 | tf_op jit(solution)/shard_map/reduce_scatter | solution.py:32
Sparse Core Ops, SparseCore 0:
  8.9 24.5 all-gather.2
  37.6 149.4 all-reduce.2
  246.1 139.2 reduce-scatter.4
  387.5 68.5 all-gather.4
  463.2 19.4 reduce-scatter.6
where the time goes:
time: 489 us
  waiting for transfers between devices  404 us (83%)
  matrix products  64.8 us (13%)
  between operations  13.2 us (3%)
  other arithmetic  6.01 us (1%)
    psum x1, waiting for transfers between devices, broadcast(): return lax.psum(kept, axis)  150 us
    reduce_scatter x1, waiting for transfers between devices, local(): lax.psum_scatter(partial_sum, 'row', scatter_dimension=0, tiled=True)  139 us
    all_gather x1, waiting for transfers between devices, local(): contracted = lax.all_gather(share, 'row', axis=0, tiled=True)  68.5 us
    dot_general x1, matrix products, local(): lax.dot_general(weighted, near, (((0,), (0,)), ((), ())), preferred_eleme...  58.8 us
    all_gather x1, waiting for transfers between devices, local(): near = lax.all_gather(orbitals, 'col', axis=0, tiled=True)  26.2 us
    reduce_scatter x1, waiting for transfers between devices, local(): lax.psum_scatter(terms.astype(jnp.bfloat16), 'col', scatter_dimension=0,...  19.6 us
  transfers between devices with their start and end apart: 5, of which 5 were waited for; matrix products, arithmetic and copies ran while one was open for 0% of the time, Pallas kernels for 0%

commit v1 on v0

--- a/solution.py
+++ b/solution.py
@@ -27,7 +27,17 @@
     share = lax.psum_scatter(partial_sum, "row", scatter_dimension=0, tiled=True).astype(
         jnp.bfloat16
     )
-    contracted = lax.all_gather(share, "row", axis=0, tiled=True)
+    lanes = lax.axis_size("row")
+    prior = sorted(((at, (at + 1) % lanes) for at in range(lanes)))
+    u_next = share
+    arrivals = [u_next]
+    for t in tuple(range(1, lanes)):
+        u_next = lax.ppermute(u_next, "row", prior)
+        arrivals.insert(0, u_next)
+    oldest = jnp.concatenate(arrivals, axis=0)
+    top = lax.axis_index("row")
+    current_value = top + 1
+    contracted = jnp.roll(oldest, current_value * share.shape[0], axis=0)
     terms = jnp.dot(interp, contracted, preferred_element_type=jnp.float32)
     return lax.psum_scatter(terms.astype(jnp.bfloat16), "col", scatter_dimension=0, tiled=True)
 

time: 489 us -> 511 us (1.045)
  waiting for transfers between devices: 404 us -> 423 us
  local copies, waits for them, and re-layouts: 0.93 us -> 6.38 us
    ppermute x0 -> x7, waiting for transfers between devices: none -> 88.7 us  [local(): u_next = lax.ppermute(u_next, 'row', prior)]
    all_gather x1 -> x0, waiting for transfers between devices: 68.5 us -> none  [local(): contracted = lax.all_gather(share, 'row', axis=0, tiled=True)]
    unnamed x3 -> x23, local copies, waits for them, and re-layouts: 0.93 us -> 6.38 us
  transfers between devices with their start and end apart: 5 -> 11, of which waited for: 5 -> 11; matrix products, arithmetic and copies ran while one was open for 0% -> 0% of each run, Pallas kernels for 0% -> 0%
where the time goes in v1:
time: 511 us
  waiting for transfers between devices  423 us (83%)
  matrix products  61.1 us (12%)
  between operations  13.3 us (3%)
  local copies, waits for them, and re-layouts  6.38 us (1%)
  other arithmetic  5.48 us (1%)
    psum x1, waiting for transfers between devices, broadcast(): return lax.psum(kept, axis)  150 us
    reduce_scatter x1, waiting for transfers between devices, local(): lax.psum_scatter(partial_sum, 'row', scatter_dimension=0, tiled=True)  139 us
    ppermute x7, waiting for transfers between devices, local(): u_next = lax.ppermute(u_next, 'row', prior)  88.7 us
    dot_general x1, matrix products, local(): lax.dot_general(weighted, near, (((0,), (0,)), ((), ())), preferred_eleme...  58.8 us
    all_gather x1, waiting for transfers between devices, local(): near = lax.all_gather(orbitals, 'col', axis=0, tiled=True)  26.2 us
    reduce_scatter x1, waiting for transfers between devices, local(): lax.psum_scatter(terms.astype(jnp.bfloat16), 'col', scatter_dimension=0,...  18.2 us
  transfers between devices with their start and end apart: 11, of which 11 were waited for; matrix products, arithmetic and copies ran while one was open for 0% of the time, Pallas kernels for 0%

profile of v1, /device:TPU:0, one launch (start us, length us, event | category | flops | bytes accessed | tf_op | source)
XLA Modules:
  0.0 510.6 jit_solution(10982703738874280928)
XLA Ops:
  6.5 0.7 all-gather.2.cloned.1.call-update
  7.3 0.0 all-reduce.3.cloned.1.call-start
  7.3 26.2 %all-gather.2.cloned.1.call-done = bf16[2560,384]{1,0:T(8,128)(2,1)} async-done(((bf16[640,384]{1,0:T(8,128)(2,1)}), bf16[2560,384]{1,0:T(8,128)(2,1)}) %all-gather.2.cloned.1.call-update) | async-done | bytes 1966096 | tf_op jit(solution)/shard_map/all_gather | solution.py:13
  33.5 4.0 broadcast_select_fusion.1
  37.4 0.0 all-reduce.3.cloned.1.call-update
  37.5 0.0 reduce-scatter.5.cloned.1.call-start
  37.5 149.6 %all-reduce.3.cloned.1.call-done = (bf16[2560,384]{1,0:T(8,128)(2,1)}, bf16[2560,384]{1,0:T(8,128)(2,1)}) async-done(((bf16[2560,384]{1,0:T(8,128)(2,1)}, bf16[2560,384]{1,0:T(8,128)(2,1)}), (bf16[2560,384]{1,0:T(8,128)(2,1)}, bf16[2560,384]{1,0:T(8,128)(2,1)})) %all-reduce.3.cloned.1.call-update) | async-done | bytes 3932176 | tf_op jit(solution)/shard_map/psum | solution.py:9
  187.1 58.8 %fusion.1 = f32[5120,384]{1,0:T(8,128)} fusion(bf16[2560,384]{1,0:T(8,128)(2,1)S(1)} %copy-done.1, f32[2560,5120]{1,0:T(8,128)} %param.4, bf16[2560,384]{1,0:T(8,128)(2,1)} %get-tuple-element.5, bf16[2560,384]{1,0:T(8,128)(2,1)} %get-tuple-element.6), kind=kOutput, calls=%fused_computation.2 | convolution fusion | flops 20166737920 | bytes 66191360 | tf_op jit(solution)/shard_map/dot_general | solution.py:24
  245.9 0.0 reduce-scatter.5.cloned.1.call-update
  245.9 0.0 reduce-scatter.7.cloned.1.call-start
  246.0 139.4 %reduce-scatter.5.cloned.1.call-done = f32[640,384]{1,0:T(8,128)} async-done(((f32[5120,384]{1,0:T(8,128)}), f32[640,384]{1,0:T(8,128)}) %reduce-scatter.5.cloned.1.call-update) | async-done | bytes 983056 | tf_op jit(solution)/shard_map/reduce_scatter | solution.py:27
  385.3 1.3 convert_element_type.16
  386.7 1.5 collective-permute-start
  388.2 13.1 %collective-permute-done = bf16[640,384]{1,0:T(8,128)(2,1)S(1)} collective-permute-done((bf16[640,384]{1,0:T(8,128)(2,1)S(1)}, bf16[640,384]{1,0:T(8,128)(2,1)S(1)}, u32[]{:S(2)}, u32[]{:S(2)}) %collective-permute-start) | collective-permute-done | bytes 491552 | tf_op jit(solution)/shard_map/ppermute | solution.py:35
  401.3 0.0 collective-permute-start.1
  401.4 13.8 %collective-permute-done.1 = bf16[640,384]{1,0:T(8,128)(2,1)S(1)} collective-permute-done((bf16[640,384]{1,0:T(8,128)(2,1)S(1)}, bf16[640,384]{1,0:T(8,128)(2,1)S(1)}, u32[]{:S(2)}, u32[]{:S(2)}) %collective-permute-start.1) | collective-permute-done | bytes 491552 | tf_op jit(solution)/shard_map/ppermute | solution.py:35
  415.1 0.0 collective-permute-start.2
  415.1 12.9 %collective-permute-done.2 = bf16[640,384]{1,0:T(8,128)(2,1)S(1)} collective-permute-done((bf16[640,384]{1,0:T(8,128)(2,1)S(1)}, bf16[640,384]{1,0:T(8,128)(2,1)S(1)}, u32[]{:S(2)}, u32[]{:S(2)}) %collective-permute-start.2) | collective-permute-done | bytes 491552 | tf_op jit(solution)/shard_map/ppermute | solution.py:35
  428.0 0.0 collective-permute-start.3
  428.0 12.1 %collective-permute-done.3 = bf16[640,384]{1,0:T(8,128)(2,1)S(1)} collective-permute-done((bf16[640,384]{1,0:T(8,128)(2,1)S(1)}, bf16[640,384]{1,0:T(8,128)(2,1)S(1)}, u32[]{:S(2)}, u32[]{:S(2)}) %collective-permute-start.3) | collective-permute-done | bytes 491552 | tf_op jit(solution)/shard_map/ppermute | solution.py:35
  440.1 0.0 collective-permute-start.4
  440.1 12.0 %collective-permute-done.4 = bf16[640,384]{1,0:T(8,128)(2,1)S(1)} collective-permute-done((bf16[640,384]{1,0:T(8,128)(2,1)S(1)}, bf16[640,384]{1,0:T(8,128)(2,1)S(1)}, u32[]{:S(2)}, u32[]{:S(2)}) %collective-permute-start.4) | collective-permute-done | bytes 491552 | tf_op jit(solution)/shard_map/ppermute | solution.py:35
  452.1 0.0 collective-permute-start.5
  452.1 12.9 %collective-permute-done.5 = bf16[640,384]{1,0:T(8,128)(2,1)} collective-permute-done((bf16[640,384]{1,0:T(8,128)(2,1)S(1)}, bf16[640,384]{1,0:T(8,128)(2,1)}, u32[]{:S(2)}, u32[]{:S(2)}) %collective-permute-start.5) | collective-permute-done | bytes 491552 | tf_op jit(solution)/shard_map/ppermute | solution.py:35
  465.0 0.0 collective-permute-start.6
  465.0 11.8 %collective-permute-done.6 = bf16[640,384]{1,0:T(8,128)(2,1)} collective-permute-done((bf16[640,384]{1,0:T(8,128)(2,1)}, bf16[640,384]{1,0:T(8,128)(2,1)}, u32[]{:S(2)}, u32[]{:S(2)}) %collective-permute-start.6) | collective-permute-done | bytes 491552 | tf_op jit(solution)/shard_map/ppermute | solution.py:35
  476.9 1.1 constant_dynamic-update-slice_fusion.15
  478.0 0.0 slice-start
  478.0 1.3 constant_dynamic-update-slice_fusion.14
  479.2 0.1 constant_dynamic-update-slice_fusion.13
  479.3 0.1 constant_dynamic-update-slice_fusion.12
  479.4 0.1 constant_dynamic-update-slice_fusion.11
  479.5 0.1 constant_dynamic-update-slice_fusion.10
  479.6 0.1 constant_dynamic-update-slice_fusion.9
  479.7 0.1 constant_dynamic-update-slice_fusion.8
  479.8 0.0 slice-start.1
  479.8 1.2 constant_dynamic-update-slice_fusion.7
  481.0 1.1 constant_dynamic-update-slice_fusion.6
  482.1 0.1 constant_dynamic-update-slice_fusion.5
  482.2 0.1 constant_dynamic-update-slice_fusion.4
  482.3 0.1 constant_dynamic-update-slice_fusion.3
  482.4 0.1 constant_dynamic-update-slice_fusion.2
  482.5 0.1 constant_dynamic-update-slice_fusion.1
  482.5 0.1 constant_dynamic-update-slice_fusion
  482.7 2.3 fusion.13
  484.9 0.9 copy.6
  485.8 0.0 reduce-scatter.7.cloned.1.call-update
  485.9 18.2 %reduce-scatter.7.cloned.1.call-done = bf16[128,384]{1,0:T(8,128)(2,1)} async-done(((bf16[512,384]{1,0:T(8,128)(2,1)}), bf16[128,384]{1,0:T(8,128)(2,1)}) %reduce-scatter.7.cloned.1.call-update) | async-done | bytes 98320 | tf_op jit(solution)/shard_map/reduce_scatter | solution.py:42
  (8 shorter events, 0.0 us)
Async XLA Ops:
  6.5 26.9 %all-gather.2.cloned.1.call-start = ((), (), s32[]{:S(2)}) async-start(), calls=%async_computation.2 | async-start | bytes 2457600 | tf_op jit(solution)/shard_map/all_gather | solution.py:13
  7.3 179.8 %all-reduce.3.cloned.1.call-start = ((), (), s32[]{:S(2)}) async-start(), calls=%async_computation.5 | async-start | bytes 7864320 | tf_op jit(solution)/shard_map/psum | solution.py:9
  33.5 153.6 %copy-start.1 = (bf16[2560,384]{1,0:T(8,128)(2,1)S(1)}, bf16[2560,384]{1,0:T(8,128)(2,1)}, u32[]{:S(2)}) copy-start(bf16[2560,384]{1,0:T(8,128)(2,1)} %all-gather.2.cloned.1.call-done) | copy-start | bytes 5898244
  37.5 347.9 %reduce-scatter.5.cloned.1.call-start = ((), (), s32[]{:S(2)}) async-start(), calls=%async_computation.3 | async-start | bytes 8847360 | tf_op jit(solution)/shard_map/reduce_scatter | solution.py:27
  245.9 258.1 %reduce-scatter.7.cloned.1.call-start = ((), (), s32[]{:S(2)}) async-start(), calls=%async_computation.4 | async-start | bytes 491520 | tf_op jit(solution)/shard_map/reduce_scatter | solution.py:42
  385.3 94.4 %copy-start = (f32[640,384]{1,0:T(8,128)S(1)}, f32[640,384]{1,0:T(8,128)}, u32[]{:S(2)}) copy-start(f32[640,384]{1,0:T(8,128)} %reduce-scatter.5.cloned.1.call-done) | copy-start | bytes 2949124
  386.7 14.7 %collective-permute-start = (bf16[640,384]{1,0:T(8,128)(2,1)S(1)}, bf16[640,384]{1,0:T(8,128)(2,1)S(1)}, u32[]{:S(2)}, u32[]{:S(2)}) collective-permute-start(bf16[640,384]{1,0:T(8,128)(2,1)S(1)} %convert_element_type.16), channel_id=1, source_target_pairs={{0,4},{4,8},{8,12},{12,16},{16,20},{20,24},{24,28},{28,0},{1,5},{5... | collective-permute-start | bytes 1474568 | tf_op jit(solution)/shard_map/ppermute | solution.py:35
  401.3 13.8 %collective-permute-start.1 = (bf16[640,384]{1,0:T(8,128)(2,1)S(1)}, bf16[640,384]{1,0:T(8,128)(2,1)S(1)}, u32[]{:S(2)}, u32[]{:S(2)}) collective-permute-start(bf16[640,384]{1,0:T(8,128)(2,1)S(1)} %collective-permute-done), channel_id=1, source_target_pairs={{0,4},{4,8},{8,12},{12,16},{16,20},{20,24},{24,28},{28,0},{1,5},{5... | collective-permute-start | bytes 1474568 | tf_op jit(solution)/shard_map/ppermute | solution.py:35
  415.1 12.9 %collective-permute-start.2 = (bf16[640,384]{1,0:T(8,128)(2,1)S(1)}, bf16[640,384]{1,0:T(8,128)(2,1)S(1)}, u32[]{:S(2)}, u32[]{:S(2)}) collective-permute-start(bf16[640,384]{1,0:T(8,128)(2,1)S(1)} %collective-permute-done.1), channel_id=1, source_target_pairs={{0,4},{4,8},{8,12},{12,16},{16,20},{20,24},{24,28},{28,0},{1,5},{5... | collective-permute-start | bytes 1474568 | tf_op jit(solution)/shard_map/ppermute | solution.py:35
  428.0 12.1 %collective-permute-start.3 = (bf16[640,384]{1,0:T(8,128)(2,1)S(1)}, bf16[640,384]{1,0:T(8,128)(2,1)S(1)}, u32[]{:S(2)}, u32[]{:S(2)}) collective-permute-start(bf16[640,384]{1,0:T(8,128)(2,1)S(1)} %collective-permute-done.2), channel_id=1, source_target_pairs={{0,4},{4,8},{8,12},{12,16},{16,20},{20,24},{24,28},{28,0},{1,5},{5... | collective-permute-start | bytes 1474568 | tf_op jit(solution)/shard_map/ppermute | solution.py:35
  440.1 12.0 %collective-permute-start.4 = (bf16[640,384]{1,0:T(8,128)(2,1)S(1)}, bf16[640,384]{1,0:T(8,128)(2,1)S(1)}, u32[]{:S(2)}, u32[]{:S(2)}) collective-permute-start(bf16[640,384]{1,0:T(8,128)(2,1)S(1)} %collective-permute-done.3), channel_id=1, source_target_pairs={{0,4},{4,8},{8,12},{12,16},{16,20},{20,24},{24,28},{28,0},{1,5},{5... | collective-permute-start | bytes 1474568 | tf_op jit(solution)/shard_map/ppermute | solution.py:35
  452.1 12.9 %collective-permute-start.5 = (bf16[640,384]{1,0:T(8,128)(2,1)S(1)}, bf16[640,384]{1,0:T(8,128)(2,1)}, u32[]{:S(2)}, u32[]{:S(2)}) collective-permute-start(bf16[640,384]{1,0:T(8,128)(2,1)S(1)} %collective-permute-done.4), channel_id=1, source_target_pairs={{0,4},{4,8},{8,12},{12,16},{16,20},{20,24},{24,28},{28,0},{1,5},{5... | collective-permute-start | bytes 1474568 | tf_op jit(solution)/shard_map/ppermute | solution.py:35
  465.0 11.8 %collective-permute-start.6 = (bf16[640,384]{1,0:T(8,128)(2,1)}, bf16[640,384]{1,0:T(8,128)(2,1)}, u32[]{:S(2)}, u32[]{:S(2)}) collective-permute-start(bf16[640,384]{1,0:T(8,128)(2,1)} %collective-permute-done.5), channel_id=1, source_target_pairs={{0,4},{4,8},{8,12},{12,16},{16,20},{20,24},{24,28},{28,0},{1,5},{5... | collective-permute-start | bytes 1474568 | tf_op jit(solution)/shard_map/ppermute | solution.py:35
  478.0 4.7 slice-start
  479.8 2.9 slice-start.1
Sparse Core Ops, SparseCore 0:
  8.9 24.5 all-gather.1
  37.6 149.4 all-reduce.2
  246.0 139.2 reduce-scatter.4
  486.0 18.0 reduce-scatter.6
